TPU v7x, 32 devices: a whole 2x2x4 slice. The times are simulated.
32 devices in a mesh: parts: 2 (over x), ctx: 16 (over z, y, core).
Axes of the slice: x: 2, y: 2, z: 4, core: 2. Of those that a mesh axis runs over, the one named last changes fastest.
Arguments:
- queries: bfloat16 [256, 8192], P(('parts', 'ctx')), parts along dimension 0, may hold values from -24 to 24
- steer_ids: int32 [256], P(('parts', 'ctx')), parts along dimension 0, may hold values from 0 to 15
- steer_table: bfloat16 [16, 8192], replicated, may hold values from -3 to 3
- kv: bfloat16 [2, 32768, 1024], P(None, ('parts', 'ctx')), parts along dimension 1, may hold values from -4 to 4
- blocks: int32 [4, 128], P('parts'), parts along dimension 0, may hold values from 0 to 255, as said below
- w_out: bfloat16 [8192, 8192], P('ctx'), may hold values from -0.0625 to 0.0625
Outputs:
- projected: bfloat16 [256, 8192], P(('parts', 'ctx')), parts along dimension 0
There are 2 independent parts, one for each index of `parts`. A program takes and returns all parts, laid end to end along the dimension named above; an argument that names none is the same for every part. Nothing has to cross between parts.
Inputs may be any that keep to these rules, and one draw needn't show every extreme that they name: Each row lists 128 distinct key blocks and always includes block 0 and block 255.
All inputs are finite; a program needn't handle non-finite values.
Results may differ from a plain program's by a relative error of at most 0.0066.
Values may be sent and summed in bfloat16 or wider, within the bound.
No kernel may reach another device: no remote copies, remote signals or barrier semaphores. Data moves between devices by JAX's collectives and lax.ppermute only.
A program may use at most 64 MiB of HBM per device.

v0:
```python
import jax
import jax.numpy as jnp
from jax import lax
from jax.sharding import PartitionSpec as P

HEADS = 64
KV_HEADS = 8
HEAD = 128
D = 8192
BLOCK = 64


def apply_steer(queries, steer_ids, steer_table):
    lookup_ids = jnp.arange(steer_table.shape[0], dtype=jnp.int32)
    one_hot = (steer_ids[:, None] == lookup_ids[None, :]).astype(jnp.bfloat16)
    lookup = jnp.dot(one_hot, steer_table, preferred_element_type=jnp.float32)
    return (queries.astype(jnp.float32) + lookup).astype(jnp.bfloat16)


def local_keep(blocks, first_block, block_count, query_count):
    block_ids = first_block + jnp.arange(block_count, dtype=jnp.int32)
    hits = jnp.any(blocks[:, :, None] == block_ids[None, None, :], axis=1)
    full = jnp.broadcast_to(
        hits[:, None, :, None], (query_count // BLOCK, BLOCK, block_count, BLOCK)
    )
    return full.reshape(query_count, block_count * BLOCK)


def group_attend(q_rows, k_rows, v_rows, keep_rows):
    scores = lax.dot_general(
        q_rows, k_rows, (((1,), (1,)), ((), ())), preferred_element_type=jnp.float32
    )
    scores = scores * HEAD ** (-0.5)
    masked = jnp.where(keep_rows, scores, jnp.float32(-1e30))
    row_peak = jnp.max(masked, axis=1)
    weights = jnp.where(keep_rows, jnp.exp(masked - row_peak[:, None]), jnp.float32(0.0))
    row_total = jnp.sum(weights, axis=1)
    probs = weights.astype(jnp.bfloat16)
    partial_out = jnp.dot(probs, v_rows, preferred_element_type=jnp.float32)
    return (row_peak, row_total, partial_out)


def partial_attention(steered, kv_piece, keep_mask):
    query_count = steered.shape[0]
    ctx_count = kv_piece.shape[1]
    group_size = HEADS // KV_HEADS
    q_groups = steered.reshape(query_count, KV_HEADS, group_size, HEAD).transpose(1, 2, 0, 3)
    q_groups = q_groups.reshape(KV_HEADS, group_size * query_count, HEAD)
    k_groups = kv_piece[0].reshape(ctx_count, KV_HEADS, HEAD).transpose(1, 0, 2)
    v_groups = kv_piece[1].reshape(ctx_count, KV_HEADS, HEAD).transpose(1, 0, 2)
    keep_rows = jnp.tile(keep_mask, (group_size, 1))

    def one_group(triple):
        return group_attend(triple[0], triple[1], triple[2], keep_rows)

    peaks, totals, outs = lax.map(one_group, (q_groups, k_groups, v_groups))
    peaks = (
        peaks.reshape(KV_HEADS, group_size, query_count)
        .transpose(2, 0, 1)
        .reshape(query_count, HEADS)
    )
    totals = (
        totals.reshape(KV_HEADS, group_size, query_count)
        .transpose(2, 0, 1)
        .reshape(query_count, HEADS)
    )
    outs = (
        outs.reshape(KV_HEADS, group_size, query_count, HEAD)
        .transpose(2, 0, 1, 3)
        .reshape(query_count, HEADS * HEAD)
    )
    return (peaks, totals, outs)


def per_device(queries, steer_ids, steer_table, kv, blocks, w_out):
    steered_local = apply_steer(queries, steer_ids, steer_table)
    steered = lax.all_gather(steered_local, "ctx", axis=0, tiled=True)
    shard_count = lax.axis_size("ctx")
    my_index = lax.axis_index("ctx")
    query_count = steered.shape[0]
    block_count = kv.shape[1] // BLOCK
    keep_mask = local_keep(blocks, my_index * block_count, block_count, query_count)
    peaks, totals, outs = partial_attention(steered, kv, keep_mask)
    stat_width = max(HEADS, shard_count)
    per_entry = D // stat_width
    col_count = D // shard_count

    def spread(values):
        return jnp.repeat(values, stat_width // HEADS, axis=1)

    got_num, got_max, got_den = (
        lax.all_to_all(outs, "ctx", split_axis=1, concat_axis=0, tiled=True),
        lax.all_to_all(spread(peaks), "ctx", split_axis=1, concat_axis=0, tiled=True),
        lax.all_to_all(spread(totals), "ctx", split_axis=1, concat_axis=0, tiled=True),
    )
    got_num = got_num.reshape(shard_count, query_count, col_count)
    got_max = got_max.reshape(shard_count, query_count, stat_width // shard_count)
    got_den = got_den.reshape(shard_count, query_count, stat_width // shard_count)
    overall = jnp.max(got_max, axis=0)
    scales = jnp.exp(got_max - overall[None])
    denominator = jnp.sum(scales * got_den, axis=0)
    numerator = jnp.sum(jnp.repeat(scales, per_entry, axis=2) * got_num, axis=0)
    attended = (numerator / jnp.repeat(denominator, per_entry, axis=1)).astype(jnp.bfloat16)
    return lax.psum_scatter(
        jnp.dot(attended, w_out, preferred_element_type=jnp.float32),
        "ctx",
        scatter_dimension=0,
        tiled=True,
    ).astype(jnp.bfloat16)


def solution(mesh):
    return jax.shard_map(
        per_device,
        mesh=mesh,
        in_specs=(
            P(("parts", "ctx"), None),
            P(("parts", "ctx")),
            P(),
            P(None, ("parts", "ctx"), None),
            P("parts", None),
            P("ctx", None),
        ),
        out_specs=P(("parts", "ctx"), None),
        check_vma=False,
    )
```

profile of v0, /device:TPU:0, one launch (start us, length us, event | category | flops | bytes accessed | tf_op | source)
XLA Modules:
  0.0 324.4 jit_solution(4779056116548888666)
XLA Ops:
  9.3 4.0 %fusion.32 = (bf16[1,1024,1024]{2,1,0:T(8,128)(2,1)S(1)}, bf16[1,1024,1024]{2,1,0:T(8,128)(2,1)}) fusion(bf16[2,1024,1024]{2,1,0:T(8,128)(2,1)} %param.11), kind=kLoop, calls=%fused_computation.38 | loop fusion | bytes 8388608 | tf_op jit(solution)/shard_map/slice | solution.py:50
  13.4 4.0 %copy.38 = bf16[1,1024,1024]{1,2,0:T(8,128)(2,1)} copy(bf16[1,1024,1024]{2,1,0:T(8,128)(2,1)} %get-tuple-element.124) | data formatting | bytes 4194304
  17.3 2.6 copy.39
  20.9 32.8 %all-gather.2.cloned.1.call-done = bf16[128,8192]{1,0:T(8,128)(2,1)} async-done(((bf16[8,8192]{1,0:T(8,128)(2,1)}), bf16[128,8192]{1,0:T(8,128)(2,1)}) %all-gather.2.cloned.1.call-update) | async-done | bytes 2097168 | tf_op jit(solution)/shard_map/all_gather | solution.py:77
  53.7 2.2 copy.41
  57.3 58.5 %while.15 = (s32[]{:T(128)}, f32[8,1024]{1,0:T(8,128)S(1)}, f32[8,1024]{1,0:T(8,128)S(1)}, f32[8,1024,128]{2,1,0:T(8,128)}, bf16[8,1024,128]{2,1,0:T(8,128)(2,1)...) while((s32[]{:T(128)}, f32[8,1024]{1,0:T(8,128)S(1)}, ...), condition=%wide.region_4.5_spmd.clone, body=%wide.region_1.4_spmd.clone.sunk | while | flops 550500352 | bytes 18253932 | solution.py:56
  59.8 3.2 fusion.46
  67.1 3.2 fusion.46
  74.4 3.2 fusion.46
  79.7 2.0 fusion.44
  81.7 3.2 fusion.46
  89.1 3.2 fusion.46
  96.4 3.2 fusion.46
  103.7 3.2 fusion.46
  111.0 3.2 fusion.46
  116.4 3.5 %all-to-all-start = ((f32[128,16,4]{0,2,1:T(4,128)}), f32[128,16,4]{0,2,1:T(4,128)S(1)}, u32[]{:S(2)}, u32[]{:S(2)}) async-start(f32[128,16,4]{0,2,1:T(4,128)} %bitcast.7), calls=%async_computation | async-start | bytes 65536 | tf_op jit(solution)/shard_map/all_to_all | solution.py:93
  120.5 6.0 %all-to-all-done = f32[128,16,4]{0,2,1:T(4,128)S(1)} async-done(((f32[128,16,4]{0,2,1:T(4,128)}), f32[128,16,4]{0,2,1:T(4,128)S(1)}, u32[]{:S(2)}, u32[]{:S(2)}) %all-to-all-start) | async-done | bytes 32800 | tf_op jit(solution)/shard_map/all_to_all | solution.py:93
  126.5 3.5 %all-to-all-start.2 = ((f32[128,16,4]{0,2,1:T(4,128)}), f32[128,16,4]{0,2,1:T(4,128)S(1)}, u32[]{:S(2)}, u32[]{:S(2)}) async-start(f32[128,16,4]{0,2,1:T(4,128)} %bitcast.15), calls=%async_computation.2 | async-start | bytes 65536 | tf_op jit(solution)/shard_map/all_to_all | solution.py:94
  130.0 5.4 %copy.35 = f32[128,8,8,128]{0,3,2,1:T(8,128)} copy(f32[128,8,8,128]{3,0,2,1:T(8,128)} %bitcast.11) | data formatting | bytes 8388608 | tf_op jit(solution)/shard_map/transpose | solution.py:69
  136.6 4.8 %all-to-all-start.1 = ((f32[128,16,512]{0,2,1:T(8,128)}), f32[128,16,512]{0,2,1:T(8,128)}, u32[]{:S(2)}, u32[]{:S(2)}) async-start(f32[128,16,512]{0,2,1:T(8,128)} %bitcast.118), calls=%async_computation.1 | async-start | bytes 8388608 | tf_op jit(solution)/shard_map/all_to_all | solution.py:92
  141.5 77.4 %all-to-all-done.1 = f32[128,16,512]{0,2,1:T(8,128)} async-done(((f32[128,16,512]{0,2,1:T(8,128)}), f32[128,16,512]{0,2,1:T(8,128)}, u32[]{:S(2)}, u32[]{:S(2)}) %all-to-all-start.1) | async-done | bytes 4194336 | tf_op jit(solution)/shard_map/all_to_all | solution.py:92
  218.9 2.5 fusion.26
  221.4 6.6 %fusion.33 = f32[128,8192]{1,0:T(8,128)} fusion(bf16[128,512]{0,1:T(8,128)(2,1)S(1)} %fusion.27, bf16[512,8192]{1,0:T(8,128)(2,1)} %param.13), kind=kOutput, calls=%fused_computation.39 | convolution fusion | flops 1073741824 | bytes 12713984 | tf_op jit(solution)/shard_map/dot_general | solution.py:105
  228.1 87.8 %reduce-scatter.2.cloned.1.call-done = f32[8,8192]{1,0:T(8,128)} async-done(((f32[128,8192]{1,0:T(8,128)}), f32[8,8192]{1,0:T(8,128)}) %reduce-scatter.2.cloned.1.call-update) | async-done | bytes 262160 | tf_op jit(solution)/shard_map/reduce_scatter | solution.py:104
  (64 shorter events, 39.6 us)
Async XLA Ops:
  6.5 1.0 copy-start
  6.5 47.2 %all-gather.2.cloned.1.call-start = ((), (), s32[]{:S(2)}) async-start(), calls=%async_computation.4 | async-start | bytes 2228224 | tf_op jit(solution)/shard_map/all_gather | solution.py:77
  13.4 6.5 %copy-start.1 = (s32[2,128]{1,0:T(2,128)S(1)}, s32[2,128]{1,0:T(2,128)}, u32[]{:S(2)}) copy-start(s32[2,128]{1,0:T(2,128)} %param.12) | copy-start | bytes 3076
  116.4 10.1 %all-to-all-start = ((f32[128,16,4]{0,2,1:T(4,128)}), f32[128,16,4]{0,2,1:T(4,128)S(1)}, u32[]{:S(2)}, u32[]{:S(2)}) async-start(f32[128,16,4]{0,2,1:T(4,128)} %bitcast.7), calls=%async_computation | async-start | bytes 65536 | tf_op jit(solution)/shard_map/all_to_all | solution.py:93
  126.5 10.1 %all-to-all-start.2 = ((f32[128,16,4]{0,2,1:T(4,128)}), f32[128,16,4]{0,2,1:T(4,128)S(1)}, u32[]{:S(2)}, u32[]{:S(2)}) async-start(f32[128,16,4]{0,2,1:T(4,128)} %bitcast.15), calls=%async_computation.2 | async-start | bytes 65536 | tf_op jit(solution)/shard_map/all_to_all | solution.py:94
  136.6 82.3 %all-to-all-start.1 = ((f32[128,16,512]{0,2,1:T(8,128)}), f32[128,16,512]{0,2,1:T(8,128)}, u32[]{:S(2)}, u32[]{:S(2)}) async-start(f32[128,16,512]{0,2,1:T(8,128)} %bitcast.118), calls=%async_computation.1 | async-start | bytes 8388608 | tf_op jit(solution)/shard_map/all_to_all | solution.py:92
  141.3 174.6 %reduce-scatter.2.cloned.1.call-start = ((), (), s32[]{:S(2)}) async-start(), calls=%async_computation.5 | async-start | bytes 4456448 | tf_op jit(solution)/shard_map/reduce_scatter | solution.py:104
Sparse Core Ops, SparseCore 0:
  9.5 44.1 all-gather.1
  228.2 87.6 reduce-scatter.1
where the time goes:
time: 326 us; the launch traced here: 324 us
  waiting for transfers between devices  205 us (63%)
  matrix products  50.6 us (16%)
  local copies, waits for them, and re-layouts  28 us (9%)
  other arithmetic  14.8 us (5%)
  between operations  13.5 us (4%)
  starting transfers between devices  11.8 us (4%)
    reduce_scatter x1, waiting for transfers between devices, per_device(): lax.psum_scatter(jnp.dot(attended, w_out, preferred_element_type=jnp.floa...  87.8 us
    all_to_all x1, waiting for transfers between devices, per_device(): lax.all_to_all(outs, 'ctx', split_axis=1, concat_axis=0, tiled=True)  77.4 us
    all_gather x1, waiting for transfers between devices, per_device(): steered = lax.all_gather(steered_local, 'ctx', axis=0, tiled=True)  32.8 us
    dot_general x8, matrix products, group_attend(): partial_out = jnp.dot(probs, v_rows, preferred_element_type=jnp.float32)  25.8 us
    dot_general x8, matrix products, group_attend(): lax.dot_general(q_rows, k_rows, (((1,), (1,)), ((), ())), preferred_eleme...  16.4 us
    unnamed x10, local copies, waits for them, and re-layouts  11.2 us
    reduce_sum x8, other arithmetic, group_attend(): row_total = jnp.sum(weights, axis=1)  10.4 us
    dot_general x1, matrix products, per_device(): jnp.dot(attended, w_out, preferred_element_type=jnp.float32)  6.63 us
  transfers between devices with their start and end apart: 5, of which 5 were waited for; matrix products, arithmetic and copies ran while one was open for 5% of the time, Pallas kernels for 0%

commit v1 on v0

--- a/solution.py
+++ b/solution.py
@@ -89,7 +89,10 @@
         return jnp.repeat(values, stat_width // HEADS, axis=1)
 
     got_num, got_max, got_den = (
-        lax.all_to_all(outs, "ctx", split_axis=1, concat_axis=0, tiled=True),
+        jnp.concatenate(
+            lax.all_to_all(jnp.stack(jnp.split(outs, lax.axis_size("ctx"), axis=1)), "ctx", 0, 0),
+            axis=0,
+        ),
         lax.all_to_all(spread(peaks), "ctx", split_axis=1, concat_axis=0, tiled=True),
         lax.all_to_all(spread(totals), "ctx", split_axis=1, concat_axis=0, tiled=True),
     )

time: 326 us -> 355 us (1.089)
  local copies, waits for them, and re-layouts: 28 us -> 54.7 us
    unnamed x10 -> x25, local copies, waits for them, and re-layouts: 11.2 us -> 36.3 us
    all_to_all x1, waiting for transfers between devices: 1.24 us -> 4.91 us  [per_device(): lax.all_to_all(spread(totals), 'ctx', split_axis=1, concat_axis=0, tiled=...]
  transfers between devices with their start and end apart: 5 -> 5, of which waited for: 5 -> 5; matrix products, arithmetic and copies ran while one was open for 5% -> 4% of each run, Pallas kernels for 0% -> 0%
where the time goes in v1:
time: 355 us; the launch traced here: 353 us
  waiting for transfers between devices  207 us (58%)
  local copies, waits for them, and re-layouts  54.7 us (15%)
  matrix products  50.6 us (14%)
  other arithmetic  14.8 us (4%)
  between operations  13.5 us (4%)
  starting transfers between devices  11.6 us (3%)
    reduce_scatter x1, waiting for transfers between devices, per_device(): lax.psum_scatter(jnp.dot(attended, w_out, preferred_element_type=jnp.floa...  87.9 us
    all_to_all x1, waiting for transfers between devices, per_device(): lax.all_to_all(jnp.stack(jnp.split(outs, lax.axis_size('ctx'), axis=1)),...  77.4 us
    unnamed x25, local copies, waits for them, and re-layouts  36.3 us
    all_gather x1, waiting for transfers between devices, per_device(): steered = lax.all_gather(steered_local, 'ctx', axis=0, tiled=True)  32.8 us
    dot_general x8, matrix products, group_attend(): partial_out = jnp.dot(probs, v_rows, preferred_element_type=jnp.float32)  25.8 us
    dot_general x8, matrix products, group_attend(): lax.dot_general(q_rows, k_rows, (((1,), (1,)), ((), ())), preferred_eleme...  16.4 us
    reduce_sum x8, other arithmetic, group_attend(): row_total = jnp.sum(weights, axis=1)  10.4 us
  transfers between devices with their start and end apart: 5, of which 5 were waited for; matrix products, arithmetic and copies ran while one was open for 4% of the time, Pallas kernels for 0%

profile of v1, /device:TPU:0, one launch (start us, length us, event | category | flops | bytes accessed | tf_op | source)
XLA Modules:
  0.0 352.9 jit_solution(2199296953665771616)
XLA Ops:
  9.3 4.0 %fusion.48 = (bf16[1,1024,1024]{2,1,0:T(8,128)(2,1)S(1)}, bf16[1,1024,1024]{2,1,0:T(8,128)(2,1)}) fusion(bf16[2,1024,1024]{2,1,0:T(8,128)(2,1)} %param.11), kind=kLoop, calls=%fused_computation.70 | loop fusion | bytes 8388608 | tf_op jit(solution)/shard_map/slice | solution.py:50
  13.3 4.0 %copy.38 = bf16[1,1024,1024]{1,2,0:T(8,128)(2,1)} copy(bf16[1,1024,1024]{2,1,0:T(8,128)(2,1)} %get-tuple-element.124) | data formatting | bytes 4194304
  17.3 2.6 copy.39
  20.9 32.8 %all-gather.2.cloned.1.call-done = bf16[128,8192]{1,0:T(8,128)(2,1)} async-done(((bf16[8,8192]{1,0:T(8,128)(2,1)}), bf16[128,8192]{1,0:T(8,128)(2,1)}) %all-gather.2.cloned.1.call-update) | async-done | bytes 2097168 | tf_op jit(solution)/shard_map/all_gather | solution.py:77
  53.7 2.2 copy.41
  57.3 58.5 %while.15 = (s32[]{:T(128)}, f32[8,1024]{1,0:T(8,128)S(1)}, f32[8,1024]{1,0:T(8,128)S(1)}, f32[8,1024,128]{2,1,0:T(8,128)}, bf16[8,1024,128]{2,1,0:T(8,128)(2,1)...) while((s32[]{:T(128)}, f32[8,1024]{1,0:T(8,128)S(1)}, ...), condition=%wide.region_4.5_spmd.clone, body=%wide.region_1.4_spmd.clone.sunk | while | flops 550500352 | bytes 18253932 | solution.py:56
  59.8 3.2 fusion.62
  67.1 3.2 fusion.62
  74.4 3.2 fusion.62
  81.8 3.2 fusion.62
  89.1 3.2 fusion.62
  96.4 3.2 fusion.62
  103.7 3.2 fusion.62
  111.0 3.2 fusion.62
  115.8 5.4 %copy.35 = f32[128,8,8,128]{0,3,2,1:T(8,128)} copy(f32[128,8,8,128]{3,0,2,1:T(8,128)} %bitcast.11) | data formatting | bytes 8388608 | tf_op jit(solution)/shard_map/transpose | solution.py:69
  145.2 3.5 all-to-all-start
  150.9 4.3 %all-to-all-done = f32[128,16,4]{0,2,1:T(4,128)S(1)} async-done(((f32[128,16,4]{0,2,1:T(4,128)}), f32[128,16,4]{0,2,1:T(4,128)S(1)}, u32[]{:S(2)}, u32[]{:S(2)}) %all-to-all-start) | async-done | bytes 32800 | tf_op jit(solution)/shard_map/all_to_all | solution.py:96
  155.2 3.5 all-to-all-start.2
  160.4 4.9 %all-to-all-done.2 = f32[128,16,4]{0,2,1:T(4,128)S(1)} async-done(((f32[128,16,4]{0,2,1:T(4,128)}), f32[128,16,4]{0,2,1:T(4,128)S(1)}, u32[]{:S(2)}, u32[]{:S(2)}) %all-to-all-start.2) | async-done | bytes 32800 | tf_op jit(solution)/shard_map/all_to_all | solution.py:97
  165.4 4.5 %all-to-all-start.1 = ((f32[16,128,512]{1,2,0:T(8,128)}), f32[16,128,512]{1,2,0:T(8,128)}, u32[]{:S(2)}, u32[]{:S(2)}) async-start(f32[16,128,512]{1,2,0:T(8,128)} %fusion.27), calls=%async_computation.1 | async-start | bytes 8388608 | tf_op jit(solution)/shard_map/all_to_all | solution.py:93
  170.0 77.4 %all-to-all-done.1 = f32[16,128,512]{1,2,0:T(8,128)} async-done(((f32[16,128,512]{1,2,0:T(8,128)}), f32[16,128,512]{1,2,0:T(8,128)}, u32[]{:S(2)}, u32[]{:S(2)}) %all-to-all-start.1) | async-done | bytes 4194336 | tf_op jit(solution)/shard_map/all_to_all | solution.py:93
  247.4 2.5 fusion.26
  249.9 6.6 %fusion.49 = f32[128,8192]{1,0:T(8,128)} fusion(bf16[128,512]{0,1:T(8,128)(2,1)S(1)} %fusion.43, bf16[512,8192]{1,0:T(8,128)(2,1)} %param.13), kind=kOutput, calls=%fused_computation.71 | convolution fusion | flops 1073741824 | bytes 12713984 | tf_op jit(solution)/shard_map/dot_general | solution.py:108
  256.6 87.9 %reduce-scatter.2.cloned.1.call-done = f32[8,8192]{1,0:T(8,128)} async-done(((f32[128,8192]{1,0:T(8,128)}), f32[8,8192]{1,0:T(8,128)}) %reduce-scatter.2.cloned.1.call-update) | async-done | bytes 262160 | tf_op jit(solution)/shard_map/reduce_scatter | solution.py:107
  (80 shorter events, 67.2 us)
Async XLA Ops:
  6.5 1.0 copy-start
  6.5 47.2 %all-gather.2.cloned.1.call-start = ((), (), s32[]{:S(2)}) async-start(), calls=%async_computation.4 | async-start | bytes 2228224 | tf_op jit(solution)/shard_map/all_gather | solution.py:77
  13.3 6.6 %copy-start.1 = (s32[2,128]{1,0:T(2,128)S(1)}, s32[2,128]{1,0:T(2,128)}, u32[]{:S(2)}) copy-start(s32[2,128]{1,0:T(2,128)} %param.12) | copy-start | bytes 3076
  145.2 10.1 %all-to-all-start = ((f32[128,16,4]{0,2,1:T(4,128)}), f32[128,16,4]{0,2,1:T(4,128)S(1)}, u32[]{:S(2)}, u32[]{:S(2)}) async-start(f32[128,16,4]{0,2,1:T(4,128)} %bitcast.7), calls=%async_computation | async-start | bytes 65536 | tf_op jit(solution)/shard_map/all_to_all | solution.py:96
  155.2 10.1 %all-to-all-start.2 = ((f32[128,16,4]{0,2,1:T(4,128)}), f32[128,16,4]{0,2,1:T(4,128)S(1)}, u32[]{:S(2)}, u32[]{:S(2)}) async-start(f32[128,16,4]{0,2,1:T(4,128)} %bitcast.30), calls=%async_computation.2 | async-start | bytes 65536 | tf_op jit(solution)/shard_map/all_to_all | solution.py:97
  165.4 82.0 %all-to-all-start.1 = ((f32[16,128,512]{1,2,0:T(8,128)}), f32[16,128,512]{1,2,0:T(8,128)}, u32[]{:S(2)}, u32[]{:S(2)}) async-start(f32[16,128,512]{1,2,0:T(8,128)} %fusion.27), calls=%async_computation.1 | async-start | bytes 8388608 | tf_op jit(solution)/shard_map/all_to_all | solution.py:93
  169.9 174.6 %reduce-scatter.2.cloned.1.call-start = ((), (), s32[]{:S(2)}) async-start(), calls=%async_computation.5 | async-start | bytes 4456448 | tf_op jit(solution)/shard_map/reduce_scatter | solution.py:107
Sparse Core Ops, SparseCore 0:
  9.5 44.1 all-gather.1
  256.7 87.7 reduce-scatter.1
